TPU v7x, 256 devices: a whole 4x4x8 slice. The times are simulated.
256 devices in a mesh: tile: 8 (over z_hi, core), view: 32 (over z_lo, y, x).
Axes of the slice: x: 4, y: 4, z: 8 (z_hi: 4, z_lo: 2; z = z_hi * 2 + z_lo), core: 2. Of those that a mesh axis runs over, the one named last changes fastest.
Arguments:
- estimate: float32 [192, 1536, 128], P('tile', 'view'), may hold values from 0.5 to 1.5
- views: float32 [6, 192, 1536, 128], P(None, 'tile', 'view'), may hold values from 0.1 to 3
- background: float32 [6], replicated, may hold values from 0.1 to 1
- psf_taps: float32 [6, 3, 11], replicated, may hold values from 0.2 to 1
- psf_lengths: int32 [6, 3], replicated, may hold values from 3 to 11, as said below
- view_offsets: int32 [6, 3], replicated, may hold values from -4 to 4, as said below
- field_rows: int32 [6, 2], replicated, may hold values from 0 to 1536, as said below
Outputs:
- restored: float32 [192, 1536, 128], P('tile', 'view')
Inputs may be any that keep to these rules, and one draw needn't show every extreme that they name: `psf_lengths`: odd; for each dimension some view has length 11. `view_offsets`: for each dimension some view has offset 4 and another -4. `field_rows`: the first column is at most 384 and the second at least 1152; some view starts at row 0 and some ends at row 1536.
All inputs are finite; a program needn't handle non-finite values.
Results may differ from a plain program's by a relative error of at most 0.0003.
Values sent between devices are 32-bit elements; how exact they have to be, the bound alone decides.
A program may use at most 64 MiB of HBM per device.

v0:
```python
import functools

import jax
import jax.numpy as jnp
from jax import lax
from jax.experimental import pallas as pl
from jax.experimental.pallas import tpu as pltpu
from jax.sharding import PartitionSpec as P

ITERS = 2
HALO = 9
TAPS = 11
MID = 5
PAD = 8
FAR = 10000
f32 = jnp.float32
bf16 = jnp.bfloat16


def split(x):
    high = x.astype(bf16)
    low = (x - high.astype(f32)).astype(bf16)
    return high, low


def iota(shape, dim):
    return lax.broadcasted_iota(jnp.int32, shape, dim)


def kernel(
    tiles, strips_count,
    est_hbm, views_hbm, level, taps, lengths, offsets, field,
    out_ref,
    est, obs, total, mid, wz, yf, ya, xf, xa, zb, gx, sh, sl,
    z_send, y_send, c_send, z_recv, y_recv, c_recv,
    load_sem, send_sem, recv_sem,
):
    count, depth, rows, lanes = obs.shape
    reach = depth + 2 * HALO
    top = depth - HALO
    side = HALO * depth
    t = lax.axis_index("tile")
    u = lax.axis_index("view")

    load_est = pltpu.make_async_copy(est_hbm, est, load_sem.at[0])
    load_est.start()
    load_obs = pltpu.make_async_copy(views_hbm, obs, load_sem.at[1])
    load_obs.start()

    def exists(dt, du):
        terms = []
        if dt < 0:
            terms.append(t > 0)
        if dt > 0:
            terms.append(t < tiles - 1)
        if du < 0:
            terms.append(u > 0)
        if du > 0:
            terms.append(u < strips_count - 1)
        return functools.reduce(jnp.logical_and, terms)

    around = [(dt, du) for dt in (-1, 0, 1) for du in (-1, 0, 1) if (dt, du) != (0, 0)]

    def place(dt, du):
        return (dt + 1) * 3 + du + 1

    barrier = pltpu.get_barrier_semaphore()
    expected = jnp.int32(0)
    for dt, du in around:
        there = exists(dt, du)
        expected = expected + there.astype(jnp.int32)

        @pl.when(there)
        def _():
            pl.semaphore_signal(
                barrier, inc=1, device_id=(t + dt, u + du), device_id_type=pl.DeviceIdType.MESH
            )

    for phase in range(2 * ITERS):
        for s in range(2):
            y_recv[phase, s, 0:PAD] = jnp.zeros((PAD, lanes), f32)
            y_recv[phase, s, PAD + side : 2 * PAD + side] = jnp.zeros((PAD, lanes), f32)
            y_send[phase, s, 0:PAD] = jnp.zeros((PAD, lanes), f32)

            @pl.when(jnp.logical_not(exists(2 * s - 1, 0)))
            def _():
                z_recv[phase, s] = jnp.zeros((HALO, rows, lanes), f32)

            @pl.when(jnp.logical_not(exists(0, 2 * s - 1)))
            def _():
                y_recv[phase, s, PAD : PAD + side] = jnp.zeros((side, lanes), f32)

            for r in range(2):
                k = 2 * s + r
                c_recv[phase, k, 0:PAD] = jnp.zeros((PAD, lanes), f32)
                c_recv[phase, k, 96:104] = jnp.zeros((8, lanes), f32)
                c_send[phase, k, 80:104] = jnp.zeros((24, lanes), f32)

                @pl.when(jnp.logical_not(exists(2 * s - 1, 2 * r - 1)))
                def _():
                    c_recv[phase, k, 8:96] = jnp.zeros((88, lanes), f32)

    def message(phase, dt, du):
        adjoint = phase % 2
        if du == 0:
            s = (dt + 1) // 2
            if adjoint:
                src = z_send.at[phase // 2, s]
            else:
                src = est.at[pl.ds(top * s, HALO)]
            dst = z_recv.at[phase, 1 - s]
        elif dt == 0:
            s = (du + 1) // 2
            src = y_send.at[phase, s, pl.ds(PAD, side)]
            dst = y_recv.at[phase, 1 - s, pl.ds(PAD, side)]
        else:
            s, r = (dt + 1) // 2, (du + 1) // 2
            if adjoint:
                src = c_send.at[phase, 2 * s + r, pl.ds(8, 88)]
            else:
                src = y_send.at[phase, r, pl.ds(PAD + s * (side - 88), 88)]
            dst = c_recv.at[phase, 2 * (1 - s) + 1 - r, pl.ds(8, 88)]
        return pltpu.make_async_remote_copy(
            src_ref=src,
            dst_ref=dst,
            send_sem=send_sem.at[phase, place(dt, du)],
            recv_sem=recv_sem.at[phase, place(dt, du)],
            device_id=(t + dt, u + du),
            device_id_type=pl.DeviceIdType.MESH,
        )

    def send(phase, which):
        for dt, du in which:
            @pl.when(exists(dt, du))
            def _():
                message(phase, dt, du).start()

    def receive(phase, which):
        for dt, du in which:
            @pl.when(exists(-dt, -du))
            def _():
                message(phase, dt, du).wait_recv()

    def sent(phase, which):
        for dt, du in which:
            @pl.when(exists(dt, du))
            def _():
                message(phase, dt, du).wait_send()

    along_z = [(-1, 0), (1, 0)]
    along_y = [(0, -1), (0, 1)]
    corners = [(-1, -1), (-1, 1), (1, -1), (1, 1)]

    def pack(phase):
        def body(p, carry):
            y_send[phase, 0, pl.ds(PAD + HALO * p, HALO)] = est[p, 0:HALO]
            y_send[phase, 1, pl.ds(PAD + HALO * p, HALO)] = est[p, rows - HALO : rows]
            return carry

        lax.fori_loop(0, depth, body, 0)

    load_est.wait()
    pack(0)
    pl.semaphore_wait(barrier, expected)
    send(0, along_z + corners + along_y)

    def weights_of(v, d):
        length = lengths[v, d]
        half = length // 2
        raw = []
        whole = jnp.float32(0)
        for j in range(TAPS):
            inside = j < length
            whole = whole + jnp.where(inside, taps[v, d, j], 0.0)
        scale = 1.0 / jnp.full((8, lanes), whole, f32)
        for j in range(TAPS):
            at = j - MID + half
            inside = jnp.logical_and(at >= 0, at < length)
            value = taps[v, d, jnp.clip(at, 0, TAPS - 1)]
            raw.append(jnp.where(inside, value, 0.0) * scale)
        return raw

    def filled(delta, raw):
        height, width = delta.shape
        parts = []
        for h in range(0, height, 8):
            row = []
            for w in range(0, width, 128):
                piece = delta[h : h + 8, w : w + 128]
                value = jnp.zeros(piece.shape, f32)
                for j in range(TAPS):
                    value = jnp.where(piece == j, raw[j][:, : piece.shape[1]], value)
                row.append(value)
            parts.append(jnp.concatenate(row, 1) if len(row) > 1 else row[0])
        return jnp.concatenate(parts, 0)

    def extended_place(k):
        low = k - rows
        high = k - rows - 16
        value = jnp.where(k < rows, k, FAR)
        value = jnp.where(jnp.logical_and(low >= 0, low < HALO), low - HALO, value)
        return jnp.where(jnp.logical_and(high >= 0, high < HALO), high + rows, value)

    wide = rows + 32

    def tables(v, carry):
        shift = offsets[v, 0] - MID
        raw = weights_of(v, 0)
        for j in range(TAPS):
            wz[v, j] = raw[j]
        raw = weights_of(v, 1)
        shift = offsets[v, 1] - MID
        col = iota((rows, 256), 1)
        seg = col // wide
        delta = extended_place(col - seg * wide) - iota((rows, 256), 0) - shift
        delta = jnp.where(seg < 3, delta, FAR)
        high, low = split(filled(delta, raw))
        yf[pl.ds(rows * v, rows)] = jnp.where(seg < 2, high.astype(f32), low.astype(f32)).astype(bf16)
        col = iota((wide, 256), 1)
        seg = col // rows
        delta = extended_place(iota((wide, 256), 0)) - (col - seg * rows) - shift
        delta = jnp.where(seg < 3, delta, FAR)
        high, low = split(filled(delta, raw))
        ya[v] = jnp.where(seg < 2, high.astype(f32), low.astype(f32)).astype(bf16)
        raw = weights_of(v, 2)
        shift = offsets[v, 2] - MID
        delta = iota((lanes, lanes), 0) - iota((lanes, lanes), 1)
        high, low = split(filled(delta - shift, raw))
        both = jnp.concatenate([high, low], 1)
        xf[v] = jnp.concatenate([both, both], 0)
        high, low = split(filled(-delta - shift, raw))
        both = jnp.concatenate([high, low], 1)
        xa[v] = jnp.concatenate([both, both], 0)
        for half in (sh, sl):
            half[v, 0:8] = jnp.zeros((8, rows, lanes), bf16)
            half[v, depth + 18 : depth + 26] = jnp.zeros((8, rows, lanes), bf16)
        return carry

    lax.fori_loop(0, count, tables, 0)
    load_obs.wait()

    def stacked(own, low, high):
        full = jnp.concatenate([own, low, high], 0)
        a, b = split(full)
        return jnp.concatenate([a, b, a], 0)

    def rows_pass(first, second, at_first, at_second):
        rhs = jnp.concatenate([stacked(*first), stacked(*second)], 1)
        out = jnp.dot(yf[:, : 3 * wide], rhs, preferred_element_type=f32)
        mid[at_first] = out[:, :lanes]
        mid[at_second] = out[:, lanes:]

    def inner_rows(phase):
        def body(n, carry):
            def load(p):
                at = PAD + HALO * p
                return est[p], y_recv[phase, 0, pl.ds(at, 16)], y_recv[phase, 1, pl.ds(at, 16)]

            rows_pass(load(2 * n), load(2 * n + 1), HALO + 2 * n, HALO + 2 * n + 1)
            return carry

        lax.fori_loop(0, depth // 2, body, 0)

    def outer_rows(phase):
        def body(n, carry):
            def load(s):
                at = PAD + HALO * n + (7 if s == 0 else 0)
                return (
                    z_recv[phase, s, n],
                    c_recv[phase, 2 * s, pl.ds(at, 16)],
                    c_recv[phase, 2 * s + 1, pl.ds(at, 16)],
                )

            rows_pass(load(0), load(1), n, HALO + depth + n)
            return carry

        lax.fori_loop(0, HALO, body, 0)

    first_row = u * rows
    span = depth // 3

    def one_view(v, carry):
        base = offsets[v, 0] + MID - 1
        w = [wz[v, j] for j in range(TAPS)]

        def forward_depth(g, carry):
            at = pl.multiple_of(16 * g, 16)
            left = pl.multiple_of(rows * v + 16 * g, 16)
            window = []
            for i in range(depth + TAPS - 1):
                block = mid[base + i, pl.ds(left, 16)]
                window.append((block[:8], block[8:]))
                if i >= TAPS - 1:
                    p = i - TAPS + 1
                    halves = []
                    for h in range(2):
                        value = w[0] * window[p][h]
                        for j in range(1, TAPS):
                            value = value + w[j] * window[p + j][h]
                        halves.append(value)
                    a, b = split(jnp.concatenate(halves, 0))
                    zb[p, pl.ds(at, 16), :lanes] = a
                    zb[p, pl.ds(at, 16), lanes:] = b
            return carry

        lax.fori_loop(0, rows // 16, forward_depth, 0)

        place_y = first_row + iota((rows, lanes), 0)
        covered = jnp.logical_and(place_y >= field[v, 0], place_y < field[v, 1])
        back = level[v]

        def along_x(c, carry):
            part = pl.ds(span * c, span)
            lhs = zb[part].reshape(span * rows, 2 * lanes)
            out = jnp.dot(lhs, xf[v], preferred_element_type=f32)
            blurred = out[:, :lanes] + out[:, lanes:]
            blurred = blurred.reshape(span, rows, lanes)
            ratio = jnp.where(covered[None], obs[v, part] / (blurred + back), 1.0)
            a, b = split(ratio.reshape(span * rows, lanes))
            out = jnp.dot(jnp.concatenate([a, b], 1), xa[v], preferred_element_type=f32)
            gx[part] = (out[:, :lanes] + out[:, lanes:]).reshape(span, rows, lanes)
            return carry

        lax.fori_loop(0, 3, along_x, 0)

        def adjoint_depth(g, carry):
            at = pl.multiple_of(16 * g, 16)
            window = {}
            for i in range(depth + TAPS - 1):
                if i < depth:
                    block = gx[i, pl.ds(at, 16)]
                    window[i] = (block[:8], block[8:])
                halves = []
                for h in range(2):
                    terms = [w[j] * window[i - j][h] for j in range(TAPS) if 0 <= i - j < depth]
                    halves.append(functools.reduce(lambda x, y: x + y, terms))
                a, b = split(jnp.concatenate(halves, 0))
                sh[v, 8 + i, pl.ds(at, 16)] = a
                sl[v, 8 + i, pl.ds(at, 16)] = b
            return carry

        lax.fori_loop(0, rows // 16, adjoint_depth, 0)
        return carry

    def rows_adjoint(first, second):
        acc = None
        for v in range(count):
            cols = []
            for p in (first, second):
                at = p + MID - 1 - offsets[v, 0]
                a, b = sh[v, at], sl[v, at]
                cols.append(jnp.concatenate([a, b, a], 0))
            out = jnp.dot(ya[v, :, : 3 * rows], jnp.concatenate(cols, 1), preferred_element_type=f32)
            acc = out if acc is None else acc + out
        return acc

    def outer_adjoint(phase):
        def body(n, carry):
            acc = rows_adjoint(n, HALO + depth + n)
            for s in range(2):
                half = acc[:, s * lanes : (s + 1) * lanes]
                z_send[phase // 2, s, n] = half[:rows]
                for r in range(2):
                    c_send[phase, 2 * s + r, pl.ds(PAD + HALO * n, 16)] = half[rows + 16 * r : rows + 16 * r + 16]
            return carry

        lax.fori_loop(0, HALO, body, 0)

    def inner_adjoint(phase):
        def body(n, carry):
            acc = rows_adjoint(HALO + 2 * n, HALO + 2 * n + 1)
            for s in range(2):
                p = 2 * n + s
                half = acc[:, s * lanes : (s + 1) * lanes]
                total[p] = half[:rows]
                for r in range(2):
                    y_send[phase, r, pl.ds(PAD + HALO * p, 16)] = half[rows + 16 * r : rows + 16 * r + 16]
            return carry

        lax.fori_loop(0, depth // 2, body, 0)

    early = iota((16, lanes), 0) < HALO
    late = iota((16, lanes), 0) >= 16 - HALO

    def update(phase, target):
        def plane(p, s, n):
            value = total[p]
            head, body, tail = value[:16], value[16 : rows - 16], value[rows - 16 :]
            head = head + jnp.where(early, y_recv[phase, 0, pl.ds(PAD + HALO * p, 16)], 0.0)
            tail = tail + jnp.where(late, y_recv[phase, 1, pl.ds(1 + HALO * p, 16)], 0.0)
            if s is not None:
                head = head + jnp.where(early, c_recv[phase, 2 * s, pl.ds(PAD + HALO * n, 16)], 0.0)
                tail = tail + jnp.where(late, c_recv[phase, 2 * s + 1, pl.ds(1 + HALO * n, 16)], 0.0)
            value = jnp.concatenate([head, body, tail], 0)
            if s is not None:
                value = value + z_recv[phase, s, n]
            target[p] = est[p] * value * (1.0 / count)

        def low(n, carry):
            plane(n, 0, n)
            return carry

        def middle(n, carry):
            plane(n, None, None)
            return carry

        def high(n, carry):
            plane(top + n, 1, n)
            return carry

        lax.fori_loop(0, HALO, low, 0)
        lax.fori_loop(HALO, top, middle, 0)
        lax.fori_loop(0, HALO, high, 0)

    for step in range(ITERS):
        ahead, back = 2 * step, 2 * step + 1
        receive(ahead, along_y)
        inner_rows(ahead)
        receive(ahead, along_z + corners)
        outer_rows(ahead)
        lax.fori_loop(0, count, one_view, 0)
        outer_adjoint(back)
        send(back, along_z + corners)
        inner_adjoint(back)
        send(back, along_y)
        receive(back, along_y + along_z + corners)
        sent(ahead, along_y + along_z + corners)
        if step < ITERS - 1:
            update(back, est)
            pack(ahead + 2)
            send(ahead + 2, along_z + corners + along_y)
        else:
            update(back, out_ref)
        sent(back, along_y + along_z + corners)


def solution(mesh):
    tiles, strips_count = mesh.shape["tile"], mesh.shape["view"]

    def on_device(estimate, views, background, psf_taps, psf_lengths, view_offsets, field_rows):
        count, depth, rows, lanes = views.shape
        reach = depth + 2 * HALO
        side = HALO * depth
        phases = 2 * ITERS
        anywhere = pl.BlockSpec(memory_space=pl.ANY)
        scalar = pl.BlockSpec(memory_space=pltpu.SMEM)
        v = pltpu.VMEM
        return pl.pallas_call(
            functools.partial(kernel, tiles, strips_count),
            out_shape=jax.ShapeDtypeStruct((depth, rows, lanes), f32),
            in_specs=[anywhere, anywhere] + [scalar] * 5,
            out_specs=pl.BlockSpec(memory_space=pltpu.VMEM),
            scratch_shapes=[
                v((depth, rows, lanes), f32),
                v((count, depth, rows, lanes), f32),
                v((depth, rows, lanes), f32),
                v((reach, count * rows, lanes), f32),
                v((count, TAPS, 8, lanes), f32),
                v((count * rows, 256), bf16),
                v((count, rows + 32, 256), bf16),
                v((count, 2 * lanes, 2 * lanes), bf16),
                v((count, 2 * lanes, 2 * lanes), bf16),
                v((depth, rows, 2 * lanes), bf16),
                v((depth, rows, lanes), f32),
                v((count, depth + 26, rows, lanes), bf16),
                v((count, depth + 26, rows, lanes), bf16),
                v((ITERS, 2, HALO, rows, lanes), f32),
                v((phases, 2, side + 2 * PAD, lanes), f32),
                v((phases, 4, 104, lanes), f32),
                v((phases, 2, HALO, rows, lanes), f32),
                v((phases, 2, side + 2 * PAD, lanes), f32),
                v((phases, 4, 104, lanes), f32),
                pltpu.SemaphoreType.DMA((2,)),
                pltpu.SemaphoreType.DMA((phases, 9)),
                pltpu.SemaphoreType.DMA((phases, 9)),
            ],
            compiler_params=pltpu.CompilerParams(
                collective_id=0, has_side_effects=True, vmem_limit_bytes=60 * 2**20
            ),
            name="deconvolve",
        )(estimate, views, background, psf_taps, psf_lengths, view_offsets, field_rows)

    return jax.shard_map(
        on_device,
        mesh=mesh,
        in_specs=(P("tile", "view", None), P(None, "tile", "view", None), P(), P(), P(), P(), P()),
        out_specs=P("tile", "view", None),
        check_vma=False,
    )
```

profile of v0, /device:TPU:97, one launch (start us, length us, event | category | flops | bytes accessed | tf_op | source)
XLA Modules:
  0.0 96.7 jit_solution(7557298438055575164)
XLA Ops:
  0.0 1.4 %copy.8.lengths = s32[6,3]{1,0:T(8,128)} copy(s32[6,3]{0,1:T(4,128)} %param.11) | data formatting | bytes 144 | tf_op args[4]
  1.4 1.4 %copy.9.offsets = s32[6,3]{1,0:T(8,128)} copy(s32[6,3]{0,1:T(4,128)} %param.12) | data formatting | bytes 144 | tf_op args[5]
  2.7 1.3 %copy.10.field = s32[6,2]{1,0:T(8,128)} copy(s32[6,2]{0,1:T(2,128)} %param.13) | data formatting | bytes 96 | tf_op args[6]
  4.1 90.8 %deconvolve.1 = f32[24,48,128]{2,1,0:T(8,128)} custom-call(f32[24,48,128]{2,1,0:T(8,128)} %est_hbm.1, f32[6,24,48,128]{3,2,1,0:T(8,128)} %views_hbm.1, f32[6]{0:T(128)} %level.1, f32[6,3,11]{2,1,0:T(4,128)} %taps.1, s32[6,3]{1,0:T(8,128)} %copy.8.lengths, s32[6,3]{1,0:T(8,128)} %copy.9.offsets, s32[6,2]{1,0:T(8,128)} %copy.10.field), custom_call_target="tpu_custom_call" | custom-call | tf_op jit(solution)/shard_map/deconvolve/pallas_call | solution.py:448
  94.8 1.9 %copy.12 = f32[24,48,128]{2,1,0:T(8,128)} copy(f32[24,48,128]{2,1,0:T(8,128)} %deconvolve.1) | data formatting | bytes 1179648
where the time goes:
time: 98.3 us; the launch traced here: 96.7 us
  Pallas kernels  90.8 us (92%)
  local copies, waits for them, and re-layouts  5.97 us (6%)
    pallas_call x1, Pallas kernels, on_device(): pl.pallas_call(functools.partial(kernel, tiles, strips_count), out_shape=...  90.8 us
    unnamed x4, local copies, waits for them, and re-layouts  5.97 us

commit v1 on v0

v1 whole, which is shorter than its diff:
```python
import functools

import jax
import jax.numpy as jnp
from jax import lax
from jax.experimental import pallas as pl
from jax.experimental.pallas import tpu as pltpu
from jax.sharding import PartitionSpec as P

ITERS = 2
HALO = 9
TAPS = 11
MID = 5
PAD = 8
FAR = 10000
f32 = jnp.float32
bf16 = jnp.bfloat16


def split(x):
    high = x.astype(bf16)
    low = (x - high.astype(f32)).astype(bf16)
    return high, low


def iota(shape, dim):
    return lax.broadcasted_iota(jnp.int32, shape, dim)


def kernel(
    tiles, strips_count,
    est_hbm, views_hbm, level, taps, lengths, offsets, field,
    out_ref,
    est, obs, wide_in, mid, back_mid, wide_out, zf_build, za_build, zf, za, yf, ya, xf, xa,
    zb, rb, gh, gl,
    z_send, y_send, c_send, z_recv, y_recv, c_recv,
    load_sem, send_sem, recv_sem,
):
    count, depth, rows, lanes = obs.shape
    reach = depth + 2 * HALO
    top = depth - HALO
    pitch = rows + 2 * HALO + 1
    planes = -(-reach // 16) * 16
    side = HALO * depth
    t = lax.axis_index("tile")
    u = lax.axis_index("view")

    load_est = pltpu.make_async_copy(est_hbm, est, load_sem.at[0])
    load_est.start()
    load_obs = pltpu.make_async_copy(views_hbm, obs, load_sem.at[1])
    load_obs.start()

    def exists(dt, du):
        terms = []
        if dt < 0:
            terms.append(t > 0)
        if dt > 0:
            terms.append(t < tiles - 1)
        if du < 0:
            terms.append(u > 0)
        if du > 0:
            terms.append(u < strips_count - 1)
        return functools.reduce(jnp.logical_and, terms)

    around = [(dt, du) for dt in (-1, 0, 1) for du in (-1, 0, 1) if (dt, du) != (0, 0)]

    def place(dt, du):
        return (dt + 1) * 3 + du + 1

    barrier = pltpu.get_barrier_semaphore()
    expected = jnp.int32(0)
    for dt, du in around:
        there = exists(dt, du)
        expected = expected + there.astype(jnp.int32)

        @pl.when(there)
        def _():
            pl.semaphore_signal(
                barrier, inc=1, device_id=(t + dt, u + du), device_id_type=pl.DeviceIdType.MESH
            )

    def message(phase, dt, du):
        adjoint = phase % 2
        if du == 0:
            s = (dt + 1) // 2
            if adjoint:
                src = z_send.at[phase // 2, s]
            else:
                src = est.at[pl.ds(top * s, HALO)]
            dst = z_recv.at[phase, 1 - s]
        elif dt == 0:
            s = (du + 1) // 2
            src = y_send.at[phase, s, pl.ds(PAD, side)]
            dst = y_recv.at[phase, 1 - s, pl.ds(PAD, side)]
        else:
            s, r = (dt + 1) // 2, (du + 1) // 2
            if adjoint:
                src = c_send.at[phase, 2 * s + r, pl.ds(8, 88)]
            else:
                src = y_send.at[phase, r, pl.ds(PAD + s * (side - 88), 88)]
            dst = c_recv.at[phase, 2 * (1 - s) + 1 - r, pl.ds(8, 88)]
        return pltpu.make_async_remote_copy(
            src_ref=src,
            dst_ref=dst,
            send_sem=send_sem.at[phase, place(dt, du)],
            recv_sem=recv_sem.at[phase, place(dt, du)],
            device_id=(t + dt, u + du),
            device_id_type=pl.DeviceIdType.MESH,
        )

    def send(phase, which):
        for dt, du in which:
            @pl.when(exists(dt, du))
            def _():
                message(phase, dt, du).start()

    def receive(phase, which):
        for dt, du in which:
            @pl.when(exists(-dt, -du))
            def _():
                message(phase, dt, du).wait_recv()

    def sent(phase, which):
        for dt, du in which:
            @pl.when(exists(dt, du))
            def _():
                message(phase, dt, du).wait_send()

    along_z = [(-1, 0), (1, 0)]
    along_y = [(0, -1), (0, 1)]
    corners = [(-1, -1), (-1, 1), (1, -1), (1, 1)]

    def pack(phase):
        def body(p, carry):
            y_send[phase, 0, pl.ds(PAD + HALO * p, HALO)] = est[p, 0:HALO]
            y_send[phase, 1, pl.ds(PAD + HALO * p, HALO)] = est[p, rows - HALO : rows]
            return carry

        lax.fori_loop(0, depth, body, 0)

    load_est.wait()
    pack(0)
    pl.semaphore_wait(barrier, expected)
    send(0, along_z + corners + along_y)

    for phase in range(2 * ITERS):
        for s in range(2):
            y_recv[phase, s, 0:PAD] = jnp.zeros((PAD, lanes), f32)
            y_recv[phase, s, PAD + side : 2 * PAD + side] = jnp.zeros((PAD, lanes), f32)
            y_send[phase, s, 0:PAD] = jnp.zeros((PAD, lanes), f32)

            @pl.when(jnp.logical_not(exists(2 * s - 1, 0)))
            def _():
                z_recv[phase, s] = jnp.zeros((HALO, rows, lanes), f32)

            @pl.when(jnp.logical_not(exists(0, 2 * s - 1)))
            def _():
                y_recv[phase, s, PAD : PAD + side] = jnp.zeros((side, lanes), f32)

            for r in range(2):
                k = 2 * s + r
                c_recv[phase, k, 0:PAD] = jnp.zeros((PAD, lanes), f32)
                c_recv[phase, k, 96:104] = jnp.zeros((8, lanes), f32)
                c_send[phase, k, 80:104] = jnp.zeros((24, lanes), f32)

                @pl.when(jnp.logical_not(exists(2 * s - 1, 2 * r - 1)))
                def _():
                    c_recv[phase, k, 8:96] = jnp.zeros((88, lanes), f32)

    def weights_of(v, d):
        length = lengths[d, v]
        half = length // 2
        raw = []
        whole = jnp.float32(0)
        for j in range(TAPS):
            inside = j < length
            whole = whole + jnp.where(inside, taps[v, d, j], 0.0)
        scale = 1.0 / jnp.full((8, lanes), whole, f32)
        for j in range(TAPS):
            at = j - MID + half
            inside = jnp.logical_and(at >= 0, at < length)
            value = taps[v, d, jnp.clip(at, 0, TAPS - 1)]
            raw.append(jnp.where(inside, value, 0.0) * scale)
        return raw

    def filled(delta, raw):
        height, width = delta.shape
        parts = []
        for h in range(0, height, 8):
            row = []
            for w in range(0, width, 128):
                piece = delta[h : h + 8, w : w + 128]
                value = jnp.zeros(piece.shape, f32)
                for j in range(TAPS):
                    value = jnp.where(piece == j, raw[j], value)
                row.append(value)
            parts.append(jnp.concatenate(row, 1) if len(row) > 1 else row[0])
        return jnp.concatenate(parts, 0)

    def segmented(delta, seg, raw):
        high, low = split(filled(jnp.where(seg < 3, delta, FAR), raw))
        return jnp.where(seg < 2, high.astype(f32), low.astype(f32))

    sums = count * depth
    tall = -(-(rows + 2 * HALO) // 16) * 16
    za_build[...] = jnp.zeros(za_build.shape, f32)

    def tables(v, carry):
        shift = offsets[0, v] + MID - 1
        raw = weights_of(v, 0)
        shape = (depth, zf_build.shape[1])
        col = iota(shape, 1)
        seg = col // planes
        zf_build[pl.ds(pl.multiple_of(depth * v, 8), depth)] = segmented(
            col - seg * planes - iota(shape, 0) - shift, seg, raw
        )
        shape = za_build.shape
        col = iota(shape, 1)
        seg = col // sums
        own = col - seg * sums
        view = own // depth
        delta = iota(shape, 0) - (own - view * depth) - shift
        za_build[...] += segmented(jnp.where(view == v, delta, FAR), seg, raw)
        raw = weights_of(v, 1)
        shift = offsets[1, v] + MID - 1
        shape = (rows, yf.shape[2])
        col = iota(shape, 1)
        seg = col // tall
        yf[v] = segmented(col - seg * tall - iota(shape, 0) - shift, seg, raw).astype(bf16)
        shape = (tall, ya.shape[2])
        col = iota(shape, 1)
        seg = col // rows
        ya[v] = segmented(iota(shape, 0) - (col - seg * rows) - shift, seg, raw).astype(bf16)
        raw = weights_of(v, 2)
        shift = offsets[2, v] - MID
        delta = iota((lanes, lanes), 0) - iota((lanes, lanes), 1)
        high, low = split(filled(delta - shift, raw))
        both = jnp.concatenate([high, low], 1)
        xf[v] = jnp.concatenate([both, both], 0)
        high, low = split(filled(-delta - shift, raw))
        both = jnp.concatenate([high, low], 1)
        xa[v] = jnp.concatenate([both, both], 0)
        return carry

    lax.fori_loop(0, count, tables, 0)
    zf[...] = zf_build[...].astype(bf16)
    za[...] = za_build[...].astype(bf16)

    def clear(n, carry):
        mid[pl.ds(pl.multiple_of(64 * n, 64), 64)] = jnp.zeros((64, lanes), f32)
        return carry

    lax.fori_loop(0, mid.shape[0] // 64, clear, 0)
    extra = wide_in.shape[0] - reach * pitch
    wide_in[reach * pitch :] = jnp.zeros((extra, lanes), f32)
    load_obs.wait()

    def tripled(x):
        a, b = split(x)
        return jnp.concatenate([a, b, a], 0)

    def gather_own():
        def body(p, carry):
            wide_in[pl.ds(pitch * (HALO + p) + HALO, rows)] = est[p]
            return carry

        lax.fori_loop(0, depth, body, 0)

    def gather_y(phase):
        def body(p, carry):
            for r in range(2):
                strip = y_recv[phase, r, pl.ds(PAD + HALO * p, HALO)]
                wide_in[pl.ds(pitch * (HALO + p) + (HALO + rows) * r, HALO)] = strip
            return carry

        lax.fori_loop(0, depth, body, 0)

    def gather_z(phase):
        def body(n, carry):
            for s in range(2):
                at = pitch * (n + (HALO + depth) * s)
                wide_in[pl.ds(at + HALO, rows)] = z_recv[phase, s, n]
                for r in range(2):
                    start = PAD + HALO * n + (7 if s == 0 else 0)
                    strip = c_recv[phase, 2 * s + r, pl.ds(start, HALO)]
                    wide_in[pl.ds(at + (HALO + rows) * r, HALO)] = strip
            return carry

        lax.fori_loop(0, HALO, body, 0)

    def forward_z(n, carry):
        for k in range(11):
            y = 22 * n + 2 * k
            pair = [tripled(wide_in[pl.ds(y + i, planes, stride=pitch)]) for i in range(2)]
            out = jnp.dot(zf[:, : 3 * planes], jnp.concatenate(pair, 1), preferred_element_type=f32)
            for i in range(2):
                mid[pl.ds(y + i, sums, stride=pitch)] = out[:, i * lanes : (i + 1) * lanes]
        return carry

    first_row = u * rows
    group = 8
    groups = depth // group

    steps = count * groups

    def spread_rows(n):
        v = n // groups
        at = depth * v + group * (n - v * groups)
        table = ya[v, :, : 3 * rows]
        for k in range(group // 2):
            pair = []
            for i in range(2):
                part = pl.ds((2 * k + i) * rows, rows)
                a, b = gh[part], gl[part]
                pair.append(jnp.concatenate([a, b, a], 0))
            out = jnp.dot(table, jnp.concatenate(pair, 1), preferred_element_type=f32)
            for i in range(2):
                back_mid[pl.ds(pitch * (at + 2 * k + i), 72)] = out[:72, i * lanes : (i + 1) * lanes]

    def spread_lanes(n):
        out = jnp.dot(rb[...], xa[n // groups], preferred_element_type=f32)
        gh[...], gl[...] = split(out[:, :lanes] + out[:, lanes:])

    def compare(n):
        v = n // groups
        c = n - v * groups
        place_y = first_row + iota((rows, lanes), 0)
        covered = jnp.logical_and(place_y >= field[0, v], place_y < field[1, v])
        back = level[v]
        out = jnp.dot(zb[...], xf[v], preferred_element_type=f32)
        for k in range(group):
            part = out[k * rows : (k + 1) * rows]
            blurred = part[:, :lanes] + part[:, lanes:]
            ratio = jnp.where(covered, obs[v, group * c + k] / (blurred + back), 1.0)
            rb[k * rows : (k + 1) * rows, :lanes], rb[k * rows : (k + 1) * rows, lanes:] = split(ratio)

    def blur_rows(n):
        v = n // groups
        at = depth * v + group * (n - v * groups)
        table = yf[v, :, : 3 * tall]
        for k in range(group // 2):
            pair = [tripled(mid[pl.ds(pitch * (at + 2 * k + i), tall)]) for i in range(2)]
            out = jnp.dot(table, jnp.concatenate(pair, 1), preferred_element_type=f32)
            for i in range(2):
                part = pl.ds((2 * k + i) * rows, rows)
                zb[part, :lanes], zb[part, lanes:] = split(out[:, i * lanes : (i + 1) * lanes])

    def middle(n, carry):
        for late_by, stage in ((3, spread_rows), (2, spread_lanes), (1, compare), (0, blur_rows)):
            stage(jnp.clip(n - late_by, 0, steps - 1))
        return carry

    def adjoint_z(n, carry):
        for k in range(11):
            y = 22 * n + 2 * k
            pair = [tripled(back_mid[pl.ds(y + i, sums, stride=pitch)]) for i in range(2)]
            out = jnp.dot(za[:, : 3 * sums], jnp.concatenate(pair, 1), preferred_element_type=f32)
            for i in range(2):
                wide_out[pl.ds(y + i, planes, stride=pitch)] = out[:, i * lanes : (i + 1) * lanes]
        return carry

    def pack_outer(phase):
        def body(n, carry):
            for s in range(2):
                at = pitch * (n + (HALO + depth) * s)
                z_send[phase // 2, s, n] = wide_out[pl.ds(at + HALO, rows)]
                for r in range(2):
                    strip = wide_out[pl.ds(at + (HALO + rows) * r, HALO)]
                    c_send[phase, 2 * s + r, pl.ds(PAD + HALO * n, HALO)] = strip
            return carry

        lax.fori_loop(0, HALO, body, 0)

    def pack_inner(phase):
        def body(p, carry):
            for r in range(2):
                strip = wide_out[pl.ds(pitch * (HALO + p) + (HALO + rows) * r, HALO)]
                y_send[phase, r, pl.ds(PAD + HALO * p, HALO)] = strip
            return carry

        lax.fori_loop(0, depth, body, 0)

    early = iota((16, lanes), 0) < HALO
    late = iota((16, lanes), 0) >= 16 - HALO

    def update(phase, target):
        def plane(p, s, n):
            value = wide_out[pl.ds(pitch * (HALO + p) + HALO, rows)]
            head, body, tail = value[:16], value[16 : rows - 16], value[rows - 16 :]
            head = head + jnp.where(early, y_recv[phase, 0, pl.ds(PAD + HALO * p, 16)], 0.0)
            tail = tail + jnp.where(late, y_recv[phase, 1, pl.ds(1 + HALO * p, 16)], 0.0)
            if s is not None:
                head = head + jnp.where(early, c_recv[phase, 2 * s, pl.ds(PAD + HALO * n, 16)], 0.0)
                tail = tail + jnp.where(late, c_recv[phase, 2 * s + 1, pl.ds(1 + HALO * n, 16)], 0.0)
            value = jnp.concatenate([head, body, tail], 0)
            if s is not None:
                value = value + z_recv[phase, s, n]
            target[p] = est[p] * value * (1.0 / count)

        def low(n, carry):
            plane(n, 0, n)
            return carry

        def central(n, carry):
            plane(n, None, None)
            return carry

        def high(n, carry):
            plane(top + n, 1, n)
            return carry

        lax.fori_loop(0, HALO, low, 0)
        lax.fori_loop(HALO, top, central, 0)
        lax.fori_loop(0, HALO, high, 0)

    for step in range(ITERS):
        ahead, back = 2 * step, 2 * step + 1
        gather_own()
        receive(ahead, along_y)
        gather_y(ahead)
        receive(ahead, along_z + corners)
        gather_z(ahead)
        lax.fori_loop(0, pitch // 22, forward_z, 0)
        lax.fori_loop(0, steps + 3, middle, 0)
        lax.fori_loop(0, pitch // 22, adjoint_z, 0)
        pack_outer(back)
        send(back, along_z + corners)
        pack_inner(back)
        send(back, along_y)
        receive(back, along_y + along_z + corners)
        sent(ahead, along_y + along_z + corners)
        if step < ITERS - 1:
            update(back, est)
            pack(ahead + 2)
            send(ahead + 2, along_z + corners + along_y)
        else:
            update(back, out_ref)
        sent(back, along_y + along_z + corners)


def solution(mesh):
    tiles, strips_count = mesh.shape["tile"], mesh.shape["view"]

    def on_device(estimate, views, background, psf_taps, psf_lengths, view_offsets, field_rows):
        count, depth, rows, lanes = views.shape
        reach = depth + 2 * HALO
        side = HALO * depth
        phases = 2 * ITERS
        pitch = rows + 2 * HALO + 1
        planes = -(-reach // 16) * 16
        tall = -(-(rows + 2 * HALO) // 16) * 16
        sums = count * depth
        anywhere = pl.BlockSpec(memory_space=pl.ANY)
        scalar = pl.BlockSpec(memory_space=pltpu.SMEM)
        v = pltpu.VMEM
        return pl.pallas_call(
            functools.partial(kernel, tiles, strips_count),
            out_shape=jax.ShapeDtypeStruct((depth, rows, lanes), f32),
            in_specs=[anywhere, anywhere] + [scalar] * 5,
            out_specs=pl.BlockSpec(memory_space=pltpu.VMEM),
            scratch_shapes=[
                v((depth, rows, lanes), f32),
                v((count, depth, rows, lanes), f32),
                v((planes * pitch + 8, lanes), f32),
                v((-(-(sums * pitch + 16) // 64) * 64, lanes), f32),
                v((sums * pitch + 16, lanes), f32),
                v((planes * pitch + 8, lanes), f32),
                v((sums, 256), f32),
                v((planes, 512), f32),
                v((sums, 256), bf16),
                v((planes, 512), bf16),
                v((count, rows, 256), bf16),
                v((count, tall, 256), bf16),
                v((count, 2 * lanes, 2 * lanes), bf16),
                v((count, 2 * lanes, 2 * lanes), bf16),
                v((8 * rows, 2 * lanes), bf16),
                v((8 * rows, 2 * lanes), bf16),
                v((8 * rows, lanes), bf16),
                v((8 * rows, lanes), bf16),
                v((ITERS, 2, HALO, rows, lanes), f32),
                v((phases, 2, side + 2 * PAD, lanes), f32),
                v((phases, 4, 104, lanes), f32),
                v((phases, 2, HALO, rows, lanes), f32),
                v((phases, 2, side + 2 * PAD, lanes), f32),
                v((phases, 4, 104, lanes), f32),
                pltpu.SemaphoreType.DMA((2,)),
                pltpu.SemaphoreType.DMA((phases, 9)),
                pltpu.SemaphoreType.DMA((phases, 9)),
            ],
            compiler_params=pltpu.CompilerParams(
                collective_id=0, has_side_effects=True, vmem_limit_bytes=60 * 2**20
            ),
            name="deconvolve",
        )(estimate, views, background, psf_taps, psf_lengths.T, view_offsets.T, field_rows.T)

    return jax.shard_map(
        on_device,
        mesh=mesh,
        in_specs=(P("tile", "view", None), P(None, "tile", "view", None), P(), P(), P(), P(), P()),
        out_specs=P("tile", "view", None),
        check_vma=False,
    )
```

time: 98.3 us -> 80 us (0.81); the launches traced: 96.7 us -> 79.8 us
  Pallas kernels: 90.8 us -> 77.9 us
  local copies, waits for them, and re-layouts: 5.97 us -> 1.92 us
    pallas_call x1, Pallas kernels: 90.8 us -> 77.9 us  [on_device(): pl.pallas_call(functools.partial(kernel, tiles, strips_count), out_shape=...]
    unnamed x4 -> x1, local copies, waits for them, and re-layouts: 5.97 us -> 1.92 us
where the time goes in v1:
time: 80 us; the launch traced here: 79.8 us
  Pallas kernels  77.9 us (97%)
  local copies, waits for them, and re-layouts  1.92 us (2%)
    pallas_call x1, Pallas kernels, on_device(): pl.pallas_call(functools.partial(kernel, tiles, strips_count), out_shape=...  77.9 us
    unnamed x1, local copies, waits for them, and re-layouts  1.92 us

profile of v1, /device:TPU:97, one launch (start us, length us, event | category | flops | bytes accessed | tf_op | source)
XLA Modules:
  0.0 79.8 jit_solution(16144557827069024180)
XLA Ops:
  0.0 77.9 %deconvolve.1 = f32[24,48,128]{2,1,0:T(8,128)} custom-call(f32[24,48,128]{2,1,0:T(8,128)} %est_hbm.1, f32[6,24,48,128]{3,2,1,0:T(8,128)} %views_hbm.1, f32[6]{0:T(128)} %level.1, f32[6,3,11]{2,1,0:T(4,128)} %taps.1, s32[3,6]{1,0:T(4,128)} %bitcast.3, s32[3,6]{1,0:T(4,128)} %bitcast.4, s32[2,6]{1,0:T(2,128)} %bitcast.5), custom_call_target="tpu_custom_call" | custom-call | tf_op jit(solution)/shard_map/deconvolve/pallas_call | solution.py:456
  77.9 1.9 %copy.9 = f32[24,48,128]{2,1,0:T(8,128)} copy(f32[24,48,128]{2,1,0:T(8,128)} %deconvolve.1) | data formatting | bytes 1179648

commit v2 on v1

--- a/solution.py
+++ b/solution.py
@@ -141,7 +141,13 @@
     load_est.wait()
     pack(0)
     pl.semaphore_wait(barrier, expected)
-    send(0, along_z + corners + along_y)
+    send(0, along_y + along_z + corners)
+
+    def blank(n, carry):
+        wide_in[pl.ds(pl.multiple_of(104 * n, 8), 104)] = jnp.zeros((104, lanes), f32)
+        return carry
+
+    lax.fori_loop(0, wide_in.shape[0] // 104, blank, 0)
 
     for phase in range(2 * ITERS):
         for s in range(2):
@@ -203,23 +209,36 @@
 
     sums = count * depth
     tall = -(-(rows + 2 * HALO) // 16) * 16
+    zf_build[...] = jnp.zeros(zf_build.shape, f32)
     za_build[...] = jnp.zeros(za_build.shape, f32)
+
+    free = depth - 2 * HALO
+    bound = 2 * HALO
+    split_at = count * free
+
+    def planes_of(m):
+        view = m // free
+        rest = m - split_at
+        late_view = rest // bound
+        place = rest - late_view * bound
+        late_own = jnp.where(place >= HALO, place + free, place)
+        inner = m < split_at
+        return jnp.where(inner, view, late_view), jnp.where(inner, HALO + m - view * free, late_own)
 
     def tables(v, carry):
         shift = offsets[0, v] + MID - 1
         raw = weights_of(v, 0)
-        shape = (depth, zf_build.shape[1])
+        shape = zf_build.shape
+        view, own = planes_of(iota(shape, 0))
         col = iota(shape, 1)
         seg = col // planes
-        zf_build[pl.ds(pl.multiple_of(depth * v, 8), depth)] = segmented(
-            col - seg * planes - iota(shape, 0) - shift, seg, raw
-        )
+        delta = col - seg * planes - own - shift
+        zf_build[...] += segmented(jnp.where(view == v, delta, FAR), seg, raw)
         shape = za_build.shape
         col = iota(shape, 1)
         seg = col // sums
-        own = col - seg * sums
-        view = own // depth
-        delta = iota(shape, 0) - (own - view * depth) - shift
+        view, own = planes_of(col - seg * sums)
+        delta = iota(shape, 0) - own - shift
         za_build[...] += segmented(jnp.where(view == v, delta, FAR), seg, raw)
         raw = weights_of(v, 1)
         shift = offsets[1, v] + MID - 1
@@ -251,8 +270,6 @@
         return carry
 
     lax.fori_loop(0, mid.shape[0] // 64, clear, 0)
-    extra = wide_in.shape[0] - reach * pitch
-    wide_in[reach * pitch :] = jnp.zeros((extra, lanes), f32)
     load_obs.wait()
 
     def tripled(x):
@@ -278,8 +295,15 @@
     def gather_z(phase):
         def body(n, carry):
             for s in range(2):
+                wide_in[pl.ds(pitch * (n + (HALO + depth) * s) + HALO, rows)] = z_recv[phase, s, n]
+            return carry
+
+        lax.fori_loop(0, HALO, body, 0)
+
+    def gather_corners(phase):
+        def body(n, carry):
+            for s in range(2):
                 at = pitch * (n + (HALO + depth) * s)
-                wide_in[pl.ds(at + HALO, rows)] = z_recv[phase, s, n]
                 for r in range(2):
                     start = PAD + HALO * n + (7 if s == 0 else 0)
                     strip = c_recv[phase, 2 * s + r, pl.ds(start, HALO)]
@@ -288,82 +312,102 @@
 
         lax.fori_loop(0, HALO, body, 0)
 
-    def forward_z(n, carry):
-        for k in range(11):
-            y = 22 * n + 2 * k
-            pair = [tripled(wide_in[pl.ds(y + i, planes, stride=pitch)]) for i in range(2)]
-            out = jnp.dot(zf[:, : 3 * planes], jnp.concatenate(pair, 1), preferred_element_type=f32)
-            for i in range(2):
-                mid[pl.ds(y + i, sums, stride=pitch)] = out[:, i * lanes : (i + 1) * lanes]
-        return carry
+    def forward_z(ys, low, high):
+        pair = [tripled(wide_in[pl.ds(y, planes, stride=pitch)]) for y in ys]
+        table = zf[low : -(-high // 16) * 16, : 3 * planes]
+        out = jnp.dot(table, jnp.concatenate(pair, 1), preferred_element_type=f32)
+        for i, y in enumerate(ys):
+            mid[pl.ds(low * pitch + y, high - low, stride=pitch)] = out[: high - low, i * lanes : (i + 1) * lanes]
+
+    def own_rows(one_pair):
+        def body(n, carry):
+            for k in range(rows // 4):
+                y = HALO + rows // 2 * n + 2 * k
+                one_pair((y, y + 1))
+            return carry
+
+        lax.fori_loop(0, 2, body, 0)
+
+    def rim_rows(one_pair):
+        for k in range(HALO):
+            one_pair((k, HALO + rows + k))
 
     first_row = u * rows
-    group = 8
-    groups = depth // group
-
-    steps = count * groups
-
-    def spread_rows(n):
-        v = n // groups
-        at = depth * v + group * (n - v * groups)
+    inner_groups = [(v, free * v, list(range(HALO, top))) for v in range(count)]
+    outer = list(range(HALO)) + list(range(top, depth))
+    outer_groups = [(v, split_at + bound * v, outer) for v in range(count)]
+    groups = inner_groups + outer_groups
+    inner_low, inner_high = 0, -(-split_at // 8) * 8
+    outer_low, outer_high = split_at // 16 * 16, sums
+
+    def spread_rows(v, at, own):
         table = ya[v, :, : 3 * rows]
-        for k in range(group // 2):
+        for k in range(0, len(own), 2):
             pair = []
             for i in range(2):
-                part = pl.ds((2 * k + i) * rows, rows)
+                part = pl.ds((k + i) * rows, rows)
                 a, b = gh[part], gl[part]
                 pair.append(jnp.concatenate([a, b, a], 0))
             out = jnp.dot(table, jnp.concatenate(pair, 1), preferred_element_type=f32)
             for i in range(2):
-                back_mid[pl.ds(pitch * (at + 2 * k + i), 72)] = out[:72, i * lanes : (i + 1) * lanes]
-
-    def spread_lanes(n):
-        out = jnp.dot(rb[...], xa[n // groups], preferred_element_type=f32)
-        gh[...], gl[...] = split(out[:, :lanes] + out[:, lanes:])
-
-    def compare(n):
-        v = n // groups
-        c = n - v * groups
+                back_mid[pl.ds(pitch * (at + k + i), 72)] = out[:72, i * lanes : (i + 1) * lanes]
+
+    def spread_lanes(v, at, own):
+        used = pl.ds(0, len(own) * rows)
+        out = jnp.dot(rb[used], xa[v], preferred_element_type=f32)
+        gh[used], gl[used] = split(out[:, :lanes] + out[:, lanes:])
+
+    def compare(v, at, own):
         place_y = first_row + iota((rows, lanes), 0)
         covered = jnp.logical_and(place_y >= field[0, v], place_y < field[1, v])
         back = level[v]
-        out = jnp.dot(zb[...], xf[v], preferred_element_type=f32)
-        for k in range(group):
+        out = jnp.dot(zb[pl.ds(0, len(own) * rows)], xf[v], preferred_element_type=f32)
+        for k, p in enumerate(own):
             part = out[k * rows : (k + 1) * rows]
             blurred = part[:, :lanes] + part[:, lanes:]
-            ratio = jnp.where(covered, obs[v, group * c + k] / (blurred + back), 1.0)
+            ratio = jnp.where(covered, obs[v, p] / (blurred + back), 1.0)
             rb[k * rows : (k + 1) * rows, :lanes], rb[k * rows : (k + 1) * rows, lanes:] = split(ratio)
 
-    def blur_rows(n):
-        v = n // groups
-        at = depth * v + group * (n - v * groups)
+    def blur_rows(v, at, own):
         table = yf[v, :, : 3 * tall]
-        for k in range(group // 2):
-            pair = [tripled(mid[pl.ds(pitch * (at + 2 * k + i), tall)]) for i in range(2)]
+        for k in range(0, len(own), 2):
+            pair = [tripled(mid[pl.ds(pitch * (at + k + i), tall)]) for i in range(2)]
             out = jnp.dot(table, jnp.concatenate(pair, 1), preferred_element_type=f32)
             for i in range(2):
-                part = pl.ds((2 * k + i) * rows, rows)
+                part = pl.ds((k + i) * rows, rows)
                 zb[part, :lanes], zb[part, lanes:] = split(out[:, i * lanes : (i + 1) * lanes])
 
-    def middle(n, carry):
-        for late_by, stage in ((3, spread_rows), (2, spread_lanes), (1, compare), (0, blur_rows)):
-            stage(jnp.clip(n - late_by, 0, steps - 1))
-        return carry
-
-    def adjoint_z(n, carry):
-        for k in range(11):
-            y = 22 * n + 2 * k
-            pair = [tripled(back_mid[pl.ds(y + i, sums, stride=pitch)]) for i in range(2)]
-            out = jnp.dot(za[:, : 3 * sums], jnp.concatenate(pair, 1), preferred_element_type=f32)
-            for i in range(2):
-                wide_out[pl.ds(y + i, planes, stride=pitch)] = out[:, i * lanes : (i + 1) * lanes]
-        return carry
+    def trips(first, last):
+        for n in range(first, last):
+            for late_by, stage in ((3, spread_rows), (2, spread_lanes), (1, compare), (0, blur_rows)):
+                if 0 <= n - late_by < len(groups):
+                    stage(*groups[n - late_by])
+
+    def inner_planes():
+        trips(0, count)
+
+    def outer_planes():
+        trips(count, len(groups) + 3)
+
+    def adjoint_z(ys):
+        pair = [tripled(back_mid[pl.ds(y, sums, stride=pitch)]) for y in ys]
+        out = jnp.dot(za[:, : 3 * sums], jnp.concatenate(pair, 1), preferred_element_type=f32)
+        for i, y in enumerate(ys):
+            wide_out[pl.ds(y, planes, stride=pitch)] = out[:, i * lanes : (i + 1) * lanes]
 
     def pack_outer(phase):
         def body(n, carry):
             for s in range(2):
                 at = pitch * (n + (HALO + depth) * s)
                 z_send[phase // 2, s, n] = wide_out[pl.ds(at + HALO, rows)]
+            return carry
+
+        lax.fori_loop(0, HALO, body, 0)
+
+    def pack_corners(phase):
+        def body(n, carry):
+            for s in range(2):
+                at = pitch * (n + (HALO + depth) * s)
                 for r in range(2):
                     strip = wide_out[pl.ds(at + (HALO + rows) * r, HALO)]
                     c_send[phase, 2 * s + r, pl.ds(PAD + HALO * n, HALO)] = strip
@@ -418,21 +462,30 @@
         gather_own()
         receive(ahead, along_y)
         gather_y(ahead)
-        receive(ahead, along_z + corners)
+        own_rows(lambda ys: forward_z(ys, inner_low, inner_high))
+        rim_rows(lambda ys: forward_z(ys, inner_low, inner_high))
+        inner_planes()
+        receive(ahead, along_z)
         gather_z(ahead)
-        lax.fori_loop(0, pitch // 22, forward_z, 0)
-        lax.fori_loop(0, steps + 3, middle, 0)
-        lax.fori_loop(0, pitch // 22, adjoint_z, 0)
+        own_rows(lambda ys: forward_z(ys, outer_low, outer_high))
+        receive(ahead, corners)
+        gather_corners(ahead)
+        rim_rows(lambda ys: forward_z(ys, outer_low, outer_high))
+        outer_planes()
+        own_rows(adjoint_z)
         pack_outer(back)
-        send(back, along_z + corners)
+        send(back, along_z)
+        rim_rows(adjoint_z)
         pack_inner(back)
         send(back, along_y)
+        pack_corners(back)
+        send(back, corners)
         receive(back, along_y + along_z + corners)
         sent(ahead, along_y + along_z + corners)
         if step < ITERS - 1:
             update(back, est)
             pack(ahead + 2)
-            send(ahead + 2, along_z + corners + along_y)
+            send(ahead + 2, along_y + along_z + corners)
         else:
             update(back, out_ref)
         sent(back, along_y + along_z + corners)
@@ -473,10 +526,10 @@
                 v((count, tall, 256), bf16),
                 v((count, 2 * lanes, 2 * lanes), bf16),
                 v((count, 2 * lanes, 2 * lanes), bf16),
-                v((8 * rows, 2 * lanes), bf16),
-                v((8 * rows, 2 * lanes), bf16),
-                v((8 * rows, lanes), bf16),
-                v((8 * rows, lanes), bf16),
+                v((2 * HALO * rows, 2 * lanes), bf16),
+                v((2 * HALO * rows, 2 * lanes), bf16),
+                v((2 * HALO * rows, lanes), bf16),
+                v((2 * HALO * rows, lanes), bf16),
                 v((ITERS, 2, HALO, rows, lanes), f32),
                 v((phases, 2, side + 2 * PAD, lanes), f32),
                 v((phases, 4, 104, lanes), f32),

time: 80 us -> 72.5 us (0.906)
  the two profiles are of different devices: /device:TPU:97 before, /device:TPU:95 now
where the time goes in v2:
time: 72.5 us; the launch traced here: 72.3 us
  Pallas kernels  70.4 us (97%)
  local copies, waits for them, and re-layouts  1.92 us (3%)
    pallas_call x1, Pallas kernels, on_device(): pl.pallas_call(functools.partial(kernel, tiles, strips_count), out_shape=...  70.4 us
    unnamed x1, local copies, waits for them, and re-layouts  1.92 us

profile of v2, /device:TPU:95, one launch (start us, length us, event | category | flops | bytes accessed | tf_op | source)
XLA Modules:
  0.0 72.3 jit_solution(18145760612583563528)
XLA Ops:
  0.0 70.4 %deconvolve.1 = f32[24,48,128]{2,1,0:T(8,128)} custom-call(f32[24,48,128]{2,1,0:T(8,128)} %est_hbm.1, f32[6,24,48,128]{3,2,1,0:T(8,128)} %views_hbm.1, f32[6]{0:T(128)} %level.1, f32[6,3,11]{2,1,0:T(4,128)} %taps.1, s32[3,6]{1,0:T(4,128)} %bitcast.3, s32[3,6]{1,0:T(4,128)} %bitcast.4, s32[2,6]{1,0:T(2,128)} %bitcast.5), custom_call_target="tpu_custom_call" | custom-call | tf_op jit(solution)/shard_map/deconvolve/pallas_call | solution.py:509
  70.4 1.9 %copy.9 = f32[24,48,128]{2,1,0:T(8,128)} copy(f32[24,48,128]{2,1,0:T(8,128)} %deconvolve.1) | data formatting | bytes 1179648

commit v3 on v2

--- a/solution.py
+++ b/solution.py
@@ -12,7 +12,8 @@
 TAPS = 11
 MID = 5
 PAD = 8
-FAR = 10000
+FAR = 100000
+STEP = 1000
 f32 = jnp.float32
 bf16 = jnp.bfloat16
 
@@ -31,9 +32,9 @@
     tiles, strips_count,
     est_hbm, views_hbm, level, taps, lengths, offsets, field,
     out_ref,
-    est, obs, wide_in, mid, back_mid, wide_out, zf_build, za_build, zf, za, yf, ya, xf, xa,
+    est, obs, wide_in, mid, back_mid, wide_out, zf_build, za_build, zf_code, za_code, yf_code, yf_seg, ya_code, ya_seg, zf, za, yf, ya, xf, xa,
     zb, rb, gh, gl,
-    z_send, y_send, c_send, z_recv, y_recv, c_recv,
+    z_send, y_send, e_send, c_send, z_recv, y_recv, e_recv, c_recv,
     load_sem, send_sem, recv_sem,
 ):
     count, depth, rows, lanes = obs.shape
@@ -50,85 +51,88 @@
     load_obs = pltpu.make_async_copy(views_hbm, obs, load_sem.at[1])
     load_obs.start()
 
-    def exists(dt, du):
-        terms = []
-        if dt < 0:
-            terms.append(t > 0)
-        if dt > 0:
-            terms.append(t < tiles - 1)
-        if du < 0:
-            terms.append(u > 0)
-        if du > 0:
-            terms.append(u < strips_count - 1)
-        return functools.reduce(jnp.logical_and, terms)
-
-    around = [(dt, du) for dt in (-1, 0, 1) for du in (-1, 0, 1) if (dt, du) != (0, 0)]
-
-    def place(dt, du):
-        return (dt + 1) * 3 + du + 1
+    above = (t > 0, t < tiles - 1)
+    beside = (u > 0, u < strips_count - 1)
+
+    def at_z(s):
+        return (t + 2 * s - 1, u)
+
+    def at_y(r):
+        return (t, u + 2 * r - 1)
 
     barrier = pltpu.get_barrier_semaphore()
     expected = jnp.int32(0)
-    for dt, du in around:
-        there = exists(dt, du)
+    for there, where in [(above[s], at_z(s)) for s in range(2)] + [(beside[r], at_y(r)) for r in range(2)]:
         expected = expected + there.astype(jnp.int32)
 
         @pl.when(there)
         def _():
-            pl.semaphore_signal(
-                barrier, inc=1, device_id=(t + dt, u + du), device_id_type=pl.DeviceIdType.MESH
-            )
-
-    def message(phase, dt, du):
+            pl.semaphore_signal(barrier, inc=1, device_id=where, device_id_type=pl.DeviceIdType.MESH)
+
+    faces_z = [("z", s, None) for s in range(2)]
+    edges = [("e", s, r) for s in range(2) for r in range(2)]
+    faces_y = [("y", None, r) for r in range(2)]
+    corners = [("c", s, r) for s in range(2) for r in range(2)]
+    names = faces_z + edges + faces_y + corners
+    inner = pl.ds(8, rows - 16)
+    strip = pl.ds(PAD, 88)
+
+    def message(phase, name):
+        kind, s, r = name
         adjoint = phase % 2
-        if du == 0:
-            s = (dt + 1) // 2
+        if kind == "z":
+            src = z_send.at[phase // 2, s, :, inner] if adjoint else est.at[pl.ds(top * s, HALO), inner]
+            dst, where = z_recv.at[phase, 1 - s, :, inner], at_z(s)
+        elif kind == "y":
+            src = y_send.at[phase, r, pl.ds(PAD, side)]
+            dst, where = y_recv.at[phase, 1 - r, pl.ds(PAD, side)], at_y(r)
+        elif kind == "e":
             if adjoint:
-                src = z_send.at[phase // 2, s]
-            else:
-                src = est.at[pl.ds(top * s, HALO)]
-            dst = z_recv.at[phase, 1 - s]
-        elif dt == 0:
-            s = (du + 1) // 2
-            src = y_send.at[phase, s, pl.ds(PAD, side)]
-            dst = y_recv.at[phase, 1 - s, pl.ds(PAD, side)]
-        else:
-            s, r = (dt + 1) // 2, (du + 1) // 2
-            if adjoint:
-                src = c_send.at[phase, 2 * s + r, pl.ds(8, 88)]
+                src = e_send.at[phase // 2, 2 * s + r, strip]
             else:
                 src = y_send.at[phase, r, pl.ds(PAD + s * (side - 88), 88)]
-            dst = c_recv.at[phase, 2 * (1 - s) + 1 - r, pl.ds(8, 88)]
+            dst, where = e_recv.at[phase, 2 * (1 - s) + r, strip], at_z(s)
+        else:
+            src = (c_send.at[phase // 2] if adjoint else e_recv.at[phase]).at[2 * s + r, strip]
+            dst, where = c_recv.at[phase, 2 * s + 1 - r, strip], at_y(r)
         return pltpu.make_async_remote_copy(
             src_ref=src,
             dst_ref=dst,
-            send_sem=send_sem.at[phase, place(dt, du)],
-            recv_sem=recv_sem.at[phase, place(dt, du)],
-            device_id=(t + dt, u + du),
+            send_sem=send_sem.at[phase, names.index(name)],
+            recv_sem=recv_sem.at[phase, names.index(name)],
+            device_id=where,
             device_id_type=pl.DeviceIdType.MESH,
         )
 
+    def outgoing(name):
+        kind, s, r = name
+        if kind == "y":
+            return beside[r]
+        return jnp.logical_and(above[s], beside[r]) if kind == "c" else above[s]
+
+    def incoming(name):
+        kind, s, r = name
+        if kind == "y":
+            return beside[1 - r]
+        return jnp.logical_and(above[s], beside[1 - r]) if kind == "c" else above[1 - s]
+
     def send(phase, which):
-        for dt, du in which:
-            @pl.when(exists(dt, du))
+        for name in which:
+            @pl.when(outgoing(name))
             def _():
-                message(phase, dt, du).start()
+                message(phase, name).start()
 
     def receive(phase, which):
-        for dt, du in which:
-            @pl.when(exists(-dt, -du))
+        for name in which:
+            @pl.when(incoming(name))
             def _():
-                message(phase, dt, du).wait_recv()
+                message(phase, name).wait_recv()
 
     def sent(phase, which):
-        for dt, du in which:
-            @pl.when(exists(dt, du))
+        for name in which:
+            @pl.when(outgoing(name))
             def _():
-                message(phase, dt, du).wait_send()
-
-    along_z = [(-1, 0), (1, 0)]
-    along_y = [(0, -1), (0, 1)]
-    corners = [(-1, -1), (-1, 1), (1, -1), (1, 1)]
+                message(phase, name).wait_send()
 
     def pack(phase):
         def body(p, carry):
@@ -141,7 +145,7 @@
     load_est.wait()
     pack(0)
     pl.semaphore_wait(barrier, expected)
-    send(0, along_y + along_z + corners)
+    send(0, edges + faces_y + faces_z)
 
     def blank(n, carry):
         wide_in[pl.ds(pl.multiple_of(104 * n, 8), 104)] = jnp.zeros((104, lanes), f32)
@@ -153,23 +157,24 @@
         for s in range(2):
             y_recv[phase, s, 0:PAD] = jnp.zeros((PAD, lanes), f32)
             y_recv[phase, s, PAD + side : 2 * PAD + side] = jnp.zeros((PAD, lanes), f32)
-            y_send[phase, s, 0:PAD] = jnp.zeros((PAD, lanes), f32)
-
-            @pl.when(jnp.logical_not(exists(2 * s - 1, 0)))
+
+            @pl.when(jnp.logical_not(above[s]))
             def _():
                 z_recv[phase, s] = jnp.zeros((HALO, rows, lanes), f32)
-
-            @pl.when(jnp.logical_not(exists(0, 2 * s - 1)))
+                for r in range(2):
+                    e_recv[phase, 2 * s + r, 8:96] = jnp.zeros((88, lanes), f32)
+
+            @pl.when(jnp.logical_not(beside[s]))
             def _():
                 y_recv[phase, s, PAD : PAD + side] = jnp.zeros((side, lanes), f32)
 
             for r in range(2):
                 k = 2 * s + r
-                c_recv[phase, k, 0:PAD] = jnp.zeros((PAD, lanes), f32)
-                c_recv[phase, k, 96:104] = jnp.zeros((8, lanes), f32)
-                c_send[phase, k, 80:104] = jnp.zeros((24, lanes), f32)
-
-                @pl.when(jnp.logical_not(exists(2 * s - 1, 2 * r - 1)))
+                for held in (e_recv, c_recv):
+                    held[phase, k, 0:PAD] = jnp.zeros((PAD, lanes), f32)
+                    held[phase, k, 96:104] = jnp.zeros((8, lanes), f32)
+
+                @pl.when(jnp.logical_not(jnp.logical_and(above[s], beside[r])))
                 def _():
                     c_recv[phase, k, 8:96] = jnp.zeros((88, lanes), f32)
 
@@ -203,9 +208,9 @@
             parts.append(jnp.concatenate(row, 1) if len(row) > 1 else row[0])
         return jnp.concatenate(parts, 0)
 
-    def segmented(delta, seg, raw):
-        high, low = split(filled(jnp.where(seg < 3, delta, FAR), raw))
-        return jnp.where(seg < 2, high.astype(f32), low.astype(f32))
+    def in_segments(value, seg):
+        high, low = split(value)
+        return jnp.where(seg < 2, high.astype(f32), low.astype(f32)).astype(bf16)
 
     sums = count * depth
     tall = -(-(rows + 2 * HALO) // 16) * 16
@@ -225,31 +230,28 @@
         inner = m < split_at
         return jnp.where(inner, view, late_view), jnp.where(inner, HALO + m - view * free, late_own)
 
+    view, own = planes_of(iota(zf_code.shape, 0))
+    col = iota(zf_code.shape, 1)
+    zf_seg = col // planes
+    zf_code[...] = jnp.where(zf_seg < 3, col - zf_seg * planes - own + STEP * view, FAR)
+    view, own = planes_of(iota(za_code.shape, 1))
+    za_code[...] = iota(za_code.shape, 0) - own + STEP * view
+    col = iota(yf_code.shape, 1)
+    yf_seg[...] = col // tall
+    yf_code[...] = jnp.where(yf_seg[...] < 3, col - yf_seg[...] * tall - iota(yf_code.shape, 0), FAR)
+    col = iota(ya_code.shape, 1)
+    ya_seg[...] = col // rows
+    ya_code[...] = jnp.where(ya_seg[...] < 3, iota(ya_code.shape, 0) - (col - ya_seg[...] * rows), FAR)
+
     def tables(v, carry):
         shift = offsets[0, v] + MID - 1
         raw = weights_of(v, 0)
-        shape = zf_build.shape
-        view, own = planes_of(iota(shape, 0))
-        col = iota(shape, 1)
-        seg = col // planes
-        delta = col - seg * planes - own - shift
-        zf_build[...] += segmented(jnp.where(view == v, delta, FAR), seg, raw)
-        shape = za_build.shape
-        col = iota(shape, 1)
-        seg = col // sums
-        view, own = planes_of(col - seg * sums)
-        delta = iota(shape, 0) - own - shift
-        za_build[...] += segmented(jnp.where(view == v, delta, FAR), seg, raw)
+        zf_build[...] += filled(zf_code[...] - (shift + STEP * v), raw)
+        za_build[...] += filled(za_code[...] - (shift + STEP * v), raw)
         raw = weights_of(v, 1)
         shift = offsets[1, v] + MID - 1
-        shape = (rows, yf.shape[2])
-        col = iota(shape, 1)
-        seg = col // tall
-        yf[v] = segmented(col - seg * tall - iota(shape, 0) - shift, seg, raw).astype(bf16)
-        shape = (tall, ya.shape[2])
-        col = iota(shape, 1)
-        seg = col // rows
-        ya[v] = segmented(iota(shape, 0) - (col - seg * rows) - shift, seg, raw).astype(bf16)
+        yf[v] = in_segments(filled(yf_code[...] - shift, raw), yf_seg[...])
+        ya[v] = in_segments(filled(ya_code[...] - shift, raw), ya_seg[...])
         raw = weights_of(v, 2)
         shift = offsets[2, v] - MID
         delta = iota((lanes, lanes), 0) - iota((lanes, lanes), 1)
@@ -261,9 +263,12 @@
         xa[v] = jnp.concatenate([both, both], 0)
         return carry
 
-    lax.fori_loop(0, count, tables, 0)
-    zf[...] = zf_build[...].astype(bf16)
-    za[...] = za_build[...].astype(bf16)
+    lax.fori_loop(0, count // 2, tables, 0)
+    receive(0, edges)
+    send(0, corners)
+    lax.fori_loop(count // 2, count, tables, 0)
+    zf[...] = in_segments(zf_build[...], zf_seg)
+    za[:planes], za[planes:] = split(za_build[...])
 
     def clear(n, carry):
         mid[pl.ds(pl.multiple_of(64 * n, 64), 64)] = jnp.zeros((64, lanes), f32)
@@ -295,7 +300,11 @@
     def gather_z(phase):
         def body(n, carry):
             for s in range(2):
-                wide_in[pl.ds(pitch * (n + (HALO + depth) * s) + HALO, rows)] = z_recv[phase, s, n]
+                at = pitch * (n + (HALO + depth) * s) + HALO
+                start = PAD + HALO * n + (7 if s == 0 else 0)
+                wide_in[pl.ds(at + 8, rows - 16)] = z_recv[phase, s, n, inner]
+                for r in range(2):
+                    wide_in[pl.ds(at + (rows - HALO) * r, HALO)] = e_recv[phase, 2 * s + r, pl.ds(start, HALO)]
             return carry
 
         lax.fori_loop(0, HALO, body, 0)
@@ -304,8 +313,8 @@
         def body(n, carry):
             for s in range(2):
                 at = pitch * (n + (HALO + depth) * s)
+                start = PAD + HALO * n + (7 if s == 0 else 0)
                 for r in range(2):
-                    start = PAD + HALO * n + (7 if s == 0 else 0)
                     strip = c_recv[phase, 2 * s + r, pl.ds(start, HALO)]
                     wide_in[pl.ds(at + (HALO + rows) * r, HALO)] = strip
             return carry
@@ -390,27 +399,41 @@
         trips(count, len(groups) + 3)
 
     def adjoint_z(ys):
-        pair = [tripled(back_mid[pl.ds(y, sums, stride=pitch)]) for y in ys]
-        out = jnp.dot(za[:, : 3 * sums], jnp.concatenate(pair, 1), preferred_element_type=f32)
+        pair = [split(back_mid[pl.ds(y, sums, stride=pitch)]) for y in ys]
+        high, low = (jnp.concatenate(part, 1) for part in zip(*pair))
+        out = jnp.dot(za[:, :sums], high, preferred_element_type=f32)
+        out = out[:planes] + out[planes:]
+        out = out + jnp.dot(za[:planes, :sums], low, preferred_element_type=f32)
         for i, y in enumerate(ys):
             wide_out[pl.ds(y, planes, stride=pitch)] = out[:, i * lanes : (i + 1) * lanes]
 
-    def pack_outer(phase):
+    def pack_outer(step):
         def body(n, carry):
             for s in range(2):
                 at = pitch * (n + (HALO + depth) * s)
-                z_send[phase // 2, s, n] = wide_out[pl.ds(at + HALO, rows)]
+                z_send[step, s, n, inner] = wide_out[pl.ds(at + HALO + 8, rows - 16)]
             return carry
 
         lax.fori_loop(0, HALO, body, 0)
 
-    def pack_corners(phase):
+    def pack_corners(step):
         def body(n, carry):
             for s in range(2):
                 at = pitch * (n + (HALO + depth) * s)
                 for r in range(2):
-                    strip = wide_out[pl.ds(at + (HALO + rows) * r, HALO)]
-                    c_send[phase, 2 * s + r, pl.ds(PAD + HALO * n, HALO)] = strip
+                    part = wide_out[pl.ds(at + (HALO + rows) * r, HALO)]
+                    c_send[step, 2 * s + r, pl.ds(PAD + HALO * n, HALO)] = part
+            return carry
+
+        lax.fori_loop(0, HALO, body, 0)
+
+    def pack_edges(phase):
+        def body(n, carry):
+            for s in range(2):
+                for r in range(2):
+                    at = pitch * (n + (HALO + depth) * s) + HALO + (rows - HALO) * r
+                    part = wide_out[pl.ds(at, HALO)] + c_recv[phase, 2 * s + r, pl.ds(PAD + HALO * n, HALO)]
+                    e_send[phase // 2, 2 * s + r, pl.ds(PAD + HALO * n, HALO)] = part
             return carry
 
         lax.fori_loop(0, HALO, body, 0)
@@ -431,14 +454,19 @@
         def plane(p, s, n):
             value = wide_out[pl.ds(pitch * (HALO + p) + HALO, rows)]
             head, body, tail = value[:16], value[16 : rows - 16], value[rows - 16 :]
-            head = head + jnp.where(early, y_recv[phase, 0, pl.ds(PAD + HALO * p, 16)], 0.0)
-            tail = tail + jnp.where(late, y_recv[phase, 1, pl.ds(1 + HALO * p, 16)], 0.0)
+            first = y_recv[phase, 0, pl.ds(PAD + HALO * p, 16)]
+            last = y_recv[phase, 1, pl.ds(1 + HALO * p, 16)]
             if s is not None:
-                head = head + jnp.where(early, c_recv[phase, 2 * s, pl.ds(PAD + HALO * n, 16)], 0.0)
-                tail = tail + jnp.where(late, c_recv[phase, 2 * s + 1, pl.ds(1 + HALO * n, 16)], 0.0)
-            value = jnp.concatenate([head, body, tail], 0)
-            if s is not None:
-                value = value + z_recv[phase, s, n]
+                first = first + e_recv[phase, 2 * s, pl.ds(PAD + HALO * n, 16)]
+                last = last + e_recv[phase, 2 * s + 1, pl.ds(1 + HALO * n, 16)]
+                near = z_recv[phase, s, n]
+                first = jnp.where(early, first, near[:16])
+                last = jnp.where(late, last, near[rows - 16 :])
+                body = body + near[16 : rows - 16]
+            else:
+                first = jnp.where(early, first, 0.0)
+                last = jnp.where(late, last, 0.0)
+            value = jnp.concatenate([head + first, body, tail + last], 0)
             target[p] = est[p] * value * (1.0 / count)
 
         def low(n, carry):
@@ -460,35 +488,41 @@
     for step in range(ITERS):
         ahead, back = 2 * step, 2 * step + 1
         gather_own()
-        receive(ahead, along_y)
+        own_rows(lambda ys: forward_z(ys, inner_low, inner_high))
+        if step > 0:
+            receive(ahead, edges)
+            send(ahead, corners)
+        receive(ahead, faces_y)
         gather_y(ahead)
-        own_rows(lambda ys: forward_z(ys, inner_low, inner_high))
         rim_rows(lambda ys: forward_z(ys, inner_low, inner_high))
         inner_planes()
-        receive(ahead, along_z)
+        receive(ahead, faces_z)
         gather_z(ahead)
         own_rows(lambda ys: forward_z(ys, outer_low, outer_high))
         receive(ahead, corners)
         gather_corners(ahead)
         rim_rows(lambda ys: forward_z(ys, outer_low, outer_high))
         outer_planes()
+        rim_rows(adjoint_z)
+        pack_corners(step)
+        send(back, corners)
         own_rows(adjoint_z)
-        pack_outer(back)
-        send(back, along_z)
-        rim_rows(adjoint_z)
+        pack_outer(step)
+        send(back, faces_z)
         pack_inner(back)
-        send(back, along_y)
-        pack_corners(back)
-        send(back, corners)
-        receive(back, along_y + along_z + corners)
-        sent(ahead, along_y + along_z + corners)
+        send(back, faces_y)
+        receive(back, corners)
+        pack_edges(back)
+        send(back, edges)
+        receive(back, faces_y + faces_z + edges)
+        sent(ahead, names)
         if step < ITERS - 1:
             update(back, est)
             pack(ahead + 2)
-            send(ahead + 2, along_y + along_z + corners)
+            send(ahead + 2, edges + faces_y + faces_z)
         else:
             update(back, out_ref)
-        sent(back, along_y + along_z + corners)
+        sent(back, names)
 
 
 def solution(mesh):
@@ -519,9 +553,15 @@
                 v((sums * pitch + 16, lanes), f32),
                 v((planes * pitch + 8, lanes), f32),
                 v((sums, 256), f32),
-                v((planes, 512), f32),
+                v((planes, 256), f32),
+                v((sums, 256), jnp.int32),
+                v((planes, 256), jnp.int32),
+                v((rows, 256), jnp.int32),
+                v((rows, 256), jnp.int32),
+                v((tall, 256), jnp.int32),
+                v((tall, 256), jnp.int32),
                 v((sums, 256), bf16),
-                v((planes, 512), bf16),
+                v((2 * planes, 256), bf16),
                 v((count, rows, 256), bf16),
                 v((count, tall, 256), bf16),
                 v((count, 2 * lanes, 2 * lanes), bf16),
@@ -532,13 +572,15 @@
                 v((2 * HALO * rows, lanes), bf16),
                 v((ITERS, 2, HALO, rows, lanes), f32),
                 v((phases, 2, side + 2 * PAD, lanes), f32),
-                v((phases, 4, 104, lanes), f32),
+                v((ITERS, 4, 104, lanes), f32),
+                v((ITERS, 4, 104, lanes), f32),
                 v((phases, 2, HALO, rows, lanes), f32),
                 v((phases, 2, side + 2 * PAD, lanes), f32),
                 v((phases, 4, 104, lanes), f32),
+                v((phases, 4, 104, lanes), f32),
                 pltpu.SemaphoreType.DMA((2,)),
-                pltpu.SemaphoreType.DMA((phases, 9)),
-                pltpu.SemaphoreType.DMA((phases, 9)),
+                pltpu.SemaphoreType.DMA((phases, 12)),
+                pltpu.SemaphoreType.DMA((phases, 12)),
             ],
             compiler_params=pltpu.CompilerParams(
                 collective_id=0, has_side_effects=True, vmem_limit_bytes=60 * 2**20

time: 72.5 us -> 67.7 us (0.934)
  the two profiles are of different devices: /device:TPU:95 before, /device:TPU:97 now
where the time goes in v3:
time: 67.7 us; the launch traced here: 67.5 us
  Pallas kernels  65.6 us (97%)
  local copies, waits for them, and re-layouts  1.92 us (3%)
    pallas_call x1, Pallas kernels, on_device(): pl.pallas_call(functools.partial(kernel, tiles, strips_count), out_shape=...  65.6 us
    unnamed x1, local copies, waits for them, and re-layouts  1.92 us

profile of v3, /device:TPU:97, one launch (start us, length us, event | category | flops | bytes accessed | tf_op | source)
XLA Modules:
  0.0 67.5 jit_solution(3707134374910323755)
XLA Ops:
  0.0 65.6 %deconvolve.1 = f32[24,48,128]{2,1,0:T(8,128)} custom-call(f32[24,48,128]{2,1,0:T(8,128)} %est_hbm.1, f32[6,24,48,128]{3,2,1,0:T(8,128)} %views_hbm.1, f32[6]{0:T(128)} %level.1, f32[6,3,11]{2,1,0:T(4,128)} %taps.1, s32[3,6]{1,0:T(4,128)} %bitcast.3, s32[3,6]{1,0:T(4,128)} %bitcast.4, s32[2,6]{1,0:T(2,128)} %bitcast.5), custom_call_target="tpu_custom_call" | custom-call | tf_op jit(solution)/shard_map/deconvolve/pallas_call | solution.py:543
  65.6 1.9 %copy.9 = f32[24,48,128]{2,1,0:T(8,128)} copy(f32[24,48,128]{2,1,0:T(8,128)} %deconvolve.1) | data formatting | bytes 1179648

commit v4 on v3

--- a/solution.py
+++ b/solution.py
@@ -506,11 +506,11 @@
         rim_rows(adjoint_z)
         pack_corners(step)
         send(back, corners)
+        pack_inner(back)
+        send(back, faces_y)
         own_rows(adjoint_z)
         pack_outer(step)
         send(back, faces_z)
-        pack_inner(back)
-        send(back, faces_y)
         receive(back, corners)
         pack_edges(back)
         send(back, edges)

time: 67.7 us -> 66.3 us (0.979)
  Pallas kernels: 65.6 us -> 64.2 us
    pallas_call x1, Pallas kernels: 65.6 us -> 64.2 us  [on_device(): pl.pallas_call(functools.partial(kernel, tiles, strips_count), out_shape=...]
where the time goes in v4:
time: 66.3 us; the launch traced here: 66.2 us
  Pallas kernels  64.2 us (97%)
  local copies, waits for them, and re-layouts  1.92 us (3%)
    pallas_call x1, Pallas kernels, on_device(): pl.pallas_call(functools.partial(kernel, tiles, strips_count), out_shape=...  64.2 us
    unnamed x1, local copies, waits for them, and re-layouts  1.92 us

profile of v4, /device:TPU:97, one launch (start us, length us, event | category | flops | bytes accessed | tf_op | source)
XLA Modules:
  0.0 66.2 jit_solution(8091711803732616921)
XLA Ops:
  0.0 64.2 %deconvolve.1 = f32[24,48,128]{2,1,0:T(8,128)} custom-call(f32[24,48,128]{2,1,0:T(8,128)} %est_hbm.1, f32[6,24,48,128]{3,2,1,0:T(8,128)} %views_hbm.1, f32[6]{0:T(128)} %level.1, f32[6,3,11]{2,1,0:T(4,128)} %taps.1, s32[3,6]{1,0:T(4,128)} %bitcast.3, s32[3,6]{1,0:T(4,128)} %bitcast.4, s32[2,6]{1,0:T(2,128)} %bitcast.5), custom_call_target="tpu_custom_call" | custom-call | tf_op jit(solution)/shard_map/deconvolve/pallas_call | solution.py:543
  64.2 1.9 %copy.9 = f32[24,48,128]{2,1,0:T(8,128)} copy(f32[24,48,128]{2,1,0:T(8,128)} %deconvolve.1) | data formatting | bytes 1179648
